TPU v7x, 32 devices: a whole 2x2x4 slice. The times are simulated.
32 devices in a mesh: cam: 4 (over x, core), pt: 8 (over z, y).
Axes of the slice: x: 2, y: 2, z: 4, core: 2. Of those that a mesh axis runs over, the one named last changes fastest.
Arguments:
- right_side: float32 [9, 65536], P(None, ('cam', 'pt')), may hold values from -6 to 6
- cam_damping: float32 [9, 65536], P(None, ('cam', 'pt')), may hold values from 0.5 to 4
- point_damping: float32 [524288], P('pt'), may hold values from 0.1 to 1
- block_ids: int32 [4, 8, 64], P('cam', 'pt'), may hold values from 0 to 255, as said below
- slab_ids: int32 [4, 8, 64], P('cam', 'pt'), may hold values from 0 to 15
- cam_index: int32 [4, 8, 64, 4096], P('cam', 'pt'), may hold values from 0 to 63
- cam_jacobian: bfloat16 [4, 8, 64, 18, 4096], P('cam', 'pt'), may hold values from -0.59765625 to 0.59765625
- point_jacobian: bfloat16 [4, 8, 64, 6, 4096], P('cam', 'pt'), may hold values from -1.796875 to 1.796875
- pair_count: int32 [4, 8], P('cam', 'pt'), may hold values from 16 to 64, as said below
Outputs:
- solution: float32 [9, 65536], P(None, ('cam', 'pt'))
- residual: float32 [9, 65536], P(None, ('cam', 'pt'))
Inputs may be any that keep to these rules, and one draw needn't show every extreme that they name: pair_count is 64 divided by a whole number from 1 to 4, rounded down; at least one device has all 64 slots used in every draw. The owner of a block is block_ids // 32; in every device's list at most 16 slots name blocks of one owner, and in every list some owner is named by exactly 16 slots.
All inputs are finite; a program needn't handle non-finite values.
Results may differ from a plain program's by a relative error of at most 0.0003.
Values sent between devices are 32-bit elements; how exact they have to be, the bound alone decides.
A program may use at most 128 MiB of HBM per device.

v0:
```python
import functools

import jax
import jax.numpy as jnp
from jax import lax
from jax.experimental import pallas as pl
from jax.experimental.pallas import tpu as pltpu
from jax.sharding import PartitionSpec as P

BLOCK = 64
ITERS = 2
LANES = 128
STEP = 8
WIDTH = 512
F32 = jnp.float32
BF16 = jnp.bfloat16
VMEM_BYTES = 56 * 1024 * 1024


def pad_rows(value, rows):
    missing = rows - value.shape[0]
    return jnp.concatenate([value, jnp.zeros((missing, value.shape[1]), value.dtype)], axis=0)


def spread_rows(source, target):
    for j in range(STEP):
        target[pl.ds(j * 8, 8), :] = jnp.broadcast_to(source[j : j + 1, :], (8, source.shape[1]))


def row_ids(rows, cols):
    return lax.broadcasted_iota(jnp.int32, (rows, cols), 0)


def forward_kernel(
    first, blocks, slabs_of, count, cam_ref, idx_ref, jc_ref, jp_ref, y_ref, proj_ref, *rest
):
    table, yacc, stage, tables, shift = rest
    step = pl.program_id(0)
    owners, _, rows, _ = cam_ref.shape
    slab_len = jc_ref.shape[2]
    parts, fields, slabs, part_len = y_ref.shape
    tall = 16 if first else 8

    @pl.when(step == 0)
    def _():
        table[...] = jnp.zeros_like(table)
        yacc[...] = jnp.zeros_like(yacc)
        stage[...] = jnp.zeros_like(stage)
        for owner in range(owners):
            for k in range(9):
                table[pl.ds(owner * rows * 16 + k, rows, stride=16), :] = cam_ref[owner, k]

    @pl.when(step * STEP < count[0])
    def _():
        for j in range(STEP):
            block = blocks[step * STEP + j]
            here = table[pl.ds(pl.multiple_of((block // 2) * 16, 16), 16), :]
            tables[pl.ds(j, 16, stride=8), :] = here
            shift[j : j + 1, :] = jnp.full((1, LANES), (block % 2) * BLOCK, jnp.int32)
        for chunk in range(slab_len // LANES):
            cols = pl.ds(chunk * LANES, LANES)
            index = idx_ref[:, cols] + shift[...]
            proj = [None, None]
            for k in range(9):
                at_camera = jnp.take_along_axis(
                    tables[pl.ds(k * 8, 8), :], index, axis=1, mode="promise_in_bounds"
                )
                for i in range(2):
                    term = jc_ref[9 * i + k, :, cols].astype(F32) * at_camera
                    proj[i] = term if k == 0 else proj[i] + term
            jp = [jp_ref[k, :, cols].astype(F32) for k in range(6)]
            made = [jp[k] * proj[0] + jp[3 + k] * proj[1] for k in range(3)]
            if first:
                pairs = [(0, 0), (1, 1), (2, 2), (0, 1), (1, 2), (0, 2)]
                made += [jp[a] * jp[b] + jp[3 + a] * jp[3 + b] for a, b in pairs]
            for i in range(2):
                proj_ref[i, :, cols] = proj[i]
            for k, value in enumerate(made):
                stage[pl.ds(chunk * 128 + k, 8, stride=16), :] = value

    def slot(j, carry):
        slab = slabs_of[step * STEP + j]
        for chunk in range(slab_len // LANES):
            spot = pl.ds(pl.multiple_of((chunk * slabs + slab) * tall, 8), tall)
            yacc[spot, :] += stage[pl.ds(pl.multiple_of(chunk * 128 + j * 16, 16), tall), :]
        return carry

    lax.fori_loop(0, jnp.clip(count[0] - step * STEP, 0, STEP), slot, 0)

    @pl.when(step == pl.num_programs(0) - 1)
    def _():
        for chunk in range(slab_len // LANES):
            part, cols = chunk * LANES // part_len, pl.ds(chunk * LANES % part_len, LANES)
            for group in range(slabs // 8):
                top = (chunk * slabs + group * 8) * tall
                for k in range(fields):
                    y_ref[part, k, pl.ds(group * 8, 8), cols] = yacc[
                        pl.ds(top + k, 8, stride=tall), :
                    ]


def backward_kernel(
    blocks, slabs_of, count, z_ref, proj_ref, idx_ref, jc_ref, jp_ref, out_ref,
    zrows, acc, spread, stage, zslot,
):
    step = pl.program_id(0)
    owners, _, rows, _ = out_ref.shape
    slab_len = jc_ref.shape[2]
    parts, _, slabs, part_len = z_ref.shape

    @pl.when(step == 0)
    def _():
        zrows[...] = jnp.zeros_like(zrows)
        acc[...] = jnp.zeros_like(acc)
        stage[...] = jnp.zeros_like(stage)
        for chunk in range(slab_len // LANES):
            part, cols = chunk * LANES // part_len, pl.ds(chunk * LANES % part_len, LANES)
            for group in range(slabs // 8):
                top = (chunk * slabs + group * 8) * 8
                for k in range(3):
                    zrows[pl.ds(top + k, 8, stride=8), :] = z_ref[
                        part, k, pl.ds(group * 8, 8), cols
                    ]

    @pl.when(step * STEP < count[0])
    def _():
        spread_rows(idx_ref, spread)
        for j in range(STEP):
            slab = slabs_of[step * STEP + j]
            for chunk in range(slab_len // LANES):
                spot = pl.ds(pl.multiple_of((chunk * slabs + slab) * 8, 8), 8)
                zslot[pl.ds(chunk * 64 + j, 8, stride=8), :] = zrows[spot, :]
        for chunk in range(slab_len // LANES):
            cols = pl.ds(chunk * LANES, LANES)
            miss = [proj_ref[i, :, cols] for i in range(2)]
            for k in range(3):
                z = zslot[pl.ds(chunk * 64 + k * 8, 8), :]
                for i in range(2):
                    miss[i] = miss[i] - jp_ref[3 * i + k, :, cols].astype(F32) * z
            for k in range(9):
                stage[pl.ds(chunk * 128 + k, 8, stride=16), :] = (
                    jc_ref[k, :, cols].astype(F32) * miss[0]
                    + jc_ref[9 + k, :, cols].astype(F32) * miss[1]
                )

    cams = row_ids(BLOCK, LANES)
    half = lax.broadcasted_iota(jnp.int32, (16, LANES), 1) // BLOCK

    def slot(j, carry):
        block = blocks[step * STEP + j]
        total = jnp.zeros((32, BLOCK), F32)
        for outer in range(0, slab_len, WIDTH):
            values = []
            hots = []
            for start in range(outer, outer + WIDTH, LANES):
                cols = pl.ds(start, LANES)
                pushed = stage[pl.ds(pl.multiple_of(start + j * 16, 16), 16), :]
                rest = pushed - pushed.astype(BF16).astype(F32)
                values.append(jnp.concatenate([pushed, rest], axis=0).astype(BF16))
                index = spread[pl.ds(pl.multiple_of(j * 8, 8), 8), cols]
                index = jnp.concatenate([index] * (BLOCK // 8), axis=0)
                hots.append(jnp.where(cams == index, 1.0, 0.0).astype(BF16))
            total = total + lax.dot_general(
                jnp.concatenate(values, axis=1),
                jnp.concatenate(hots, axis=1),
                (((1,), (1,)), ((), ())),
                preferred_element_type=F32,
            )
        sums = total[0:16] + total[16:32]
        wide = jnp.concatenate([sums, sums], axis=1)
        where = pl.ds(pl.multiple_of((block // 2) * 16, 16), 16)
        acc[where, :] += jnp.where(half == block % 2, wide, jnp.zeros_like(wide))
        return carry

    lax.fori_loop(0, jnp.clip(count[0] - step * STEP, 0, STEP), slot, 0)

    @pl.when(step == pl.num_programs(0) - 1)
    def _():
        for owner in range(owners):
            for k in range(9):
                out_ref[owner, k] = acc[pl.ds(owner * rows * 16 + k, rows, stride=16), :]


def whole(shape):
    return pl.BlockSpec(shape, lambda i, *_: (0,) * len(shape))


def data_specs(pairs, slab_len):
    return [
        pl.BlockSpec((STEP, slab_len), lambda i, *_: (i, 0)),
        pl.BlockSpec((18, STEP, slab_len), lambda i, *_: (0, i, 0)),
        pl.BlockSpec((6, STEP, slab_len), lambda i, *_: (0, i, 0)),
    ]


def forward(first, lists, cams, idx, jc, jp, parts, slabs):
    pairs, slab_len = idx.shape
    owners, _, rows, _ = cams.shape
    part_len = slab_len // parts
    y_shape = (parts, 9 if first else 3, slabs, part_len)
    proj_spec = pl.BlockSpec((2, STEP, slab_len), lambda i, *_: (0, i, 0))
    out_shape = [
        jax.ShapeDtypeStruct(y_shape, F32),
        jax.ShapeDtypeStruct((2, pairs, slab_len), F32),
    ]
    out_specs = [whole(y_shape), proj_spec]
    scratch = [
        pltpu.VMEM((owners * rows * 16, LANES), F32),
        pltpu.VMEM((slabs * (16 if first else 8) * (slab_len // LANES), LANES), F32),
        pltpu.VMEM((slab_len, LANES), F32),
        pltpu.VMEM((16 * STEP, LANES), F32),
        pltpu.VMEM((STEP, LANES), jnp.int32),
    ]
    return pl.pallas_call(
        functools.partial(forward_kernel, first),
        name="forward_first" if first else "forward_next",
        out_shape=out_shape,
        grid_spec=pltpu.PrefetchScalarGridSpec(
            num_scalar_prefetch=3,
            grid=(pairs // STEP,),
            in_specs=[whole(cams.shape)] + data_specs(pairs, slab_len),
            out_specs=out_specs,
            scratch_shapes=scratch,
        ),
        compiler_params=pltpu.CompilerParams(
            dimension_semantics=("arbitrary",), vmem_limit_bytes=VMEM_BYTES
        ),
    )(*lists, cams, idx, jc, jp)


def backward(lists, z, proj, idx, jc, jp, owners, rows):
    pairs, slab_len = idx.shape
    slabs = z.shape[2]
    out_shape = (owners, 9, rows, LANES)
    proj_spec = pl.BlockSpec((2, STEP, slab_len), lambda i, *_: (0, i, 0))
    return pl.pallas_call(
        backward_kernel,
        name="backward",
        out_shape=jax.ShapeDtypeStruct(out_shape, F32),
        grid_spec=pltpu.PrefetchScalarGridSpec(
            num_scalar_prefetch=3,
            grid=(pairs // STEP,),
            in_specs=[whole(z.shape), proj_spec] + data_specs(pairs, slab_len),
            out_specs=whole(out_shape),
            scratch_shapes=[
                pltpu.VMEM((slabs * 8 * (slab_len // LANES), LANES), F32),
                pltpu.VMEM((owners * rows * 16, LANES), F32),
                pltpu.VMEM((STEP * 8, slab_len), jnp.int32),
                pltpu.VMEM((slab_len, LANES), F32),
                pltpu.VMEM((slab_len // 2, LANES), F32),
            ],
        ),
        compiler_params=pltpu.CompilerParams(
            dimension_semantics=("arbitrary",), vmem_limit_bytes=VMEM_BYTES
        ),
    )(*lists, z, proj, idx, jc, jp)


def swap_kernel(axis, gather, x_ref, out_ref, slots, send_sem, recv_sem):
    peers = lax.axis_size(axis)
    me = lax.axis_index(axis)
    barrier = pltpu.get_barrier_semaphore()
    for hop in range(1, peers):
        pl.semaphore_signal(
            barrier,
            inc=1,
            device_id={axis: lax.rem(me + hop, peers)},
            device_id_type=pl.DeviceIdType.MESH,
        )
    pl.semaphore_wait(barrier, peers - 1)
    copies = []
    for hop in range(1, peers):
        peer = lax.rem(me + hop, peers)
        copy = pltpu.make_async_remote_copy(
            src_ref=x_ref if gather else x_ref.at[peer],
            dst_ref=slots.at[hop - 1],
            send_sem=send_sem.at[hop - 1],
            recv_sem=recv_sem.at[hop - 1],
            device_id={axis: peer},
            device_id_type=pl.DeviceIdType.MESH,
        )
        copy.start()
        copies.append(copy)
    if gather:
        out_ref[me] = x_ref[...]
        for hop in range(1, peers):
            copies[hop - 1].wait()
            out_ref[lax.rem(me + peers - hop, peers)] = slots[hop - 1]
    else:
        for copy in copies:
            copy.wait()
        for k in range(out_ref.shape[0]):
            total = x_ref[me, k]
            for hop in range(1, peers):
                total = total + slots[hop - 1, k]
            out_ref[k] = total


def swap(value, axis, gather, ident):
    peers = lax.axis_size(axis)
    piece = value.shape if gather else value.shape[1:]
    out = (peers,) + piece if gather else piece
    return pl.pallas_call(
        functools.partial(swap_kernel, axis, gather),
        name=("gather_" if gather else "scatter_") + axis,
        out_shape=jax.ShapeDtypeStruct(out, F32),
        in_specs=[pl.BlockSpec(memory_space=pltpu.VMEM)],
        out_specs=pl.BlockSpec(memory_space=pltpu.VMEM),
        scratch_shapes=[
            pltpu.VMEM((peers - 1,) + piece, F32),
            pltpu.SemaphoreType.DMA((peers - 1,)),
            pltpu.SemaphoreType.DMA((peers - 1,)),
        ],
        compiler_params=pltpu.CompilerParams(
            collective_id=ident, has_side_effects=True, vmem_limit_bytes=24 * 1024 * 1024
        ),
    )(value)


def tile_of(values):
    return jnp.broadcast_to(jnp.stack(values)[:, None, None], (len(values), 8, LANES))


def over_cam(values):
    padded = values + [jnp.zeros((), F32)] * (2 - len(values))
    return jnp.sum(swap(tile_of(padded), "cam", True, 6)[:, :, 0, 0], axis=0)


def over_pt(value):
    return jnp.sum(swap(tile_of([value]), "pt", True, 5)[:, 0, 0, 0])


def invert_points(hess, damping):
    entry_xx = hess[0] + damping
    entry_yy = hess[1] + damping
    entry_zz = hess[2] + damping
    entry_xy = hess[3]
    entry_yz = hess[4]
    entry_xz = hess[5]
    cof_xx = entry_yy * entry_zz - entry_yz * entry_yz
    cof_xy = entry_xz * entry_yz - entry_xy * entry_zz
    cof_xz = entry_xy * entry_yz - entry_xz * entry_yy
    cof_yy = entry_xx * entry_zz - entry_xz * entry_xz
    cof_yz = entry_xy * entry_xz - entry_xx * entry_yz
    cof_zz = entry_xx * entry_yy - entry_xy * entry_xy
    determinant = entry_xx * cof_xx + entry_xy * cof_xy + entry_xz * cof_xz
    return [
        cof / determinant for cof in (cof_xx, cof_xy, cof_xz, cof_yy, cof_yz, cof_zz)
    ]


def apply_inverse(inverse, vector):
    out_x = inverse[0] * vector[0] + inverse[1] * vector[1] + inverse[2] * vector[2]
    out_y = inverse[1] * vector[0] + inverse[3] * vector[1] + inverse[4] * vector[2]
    out_z = inverse[2] * vector[0] + inverse[4] * vector[1] + inverse[5] * vector[2]
    return jnp.stack([out_x, out_y, out_z])


def per_device(
    right_side,
    cam_damping,
    point_damping,
    block_ids,
    slab_ids,
    cam_index,
    cam_jacobian,
    point_jacobian,
    pair_count,
):
    pairs = block_ids.shape[2]
    slab_len = cam_index.shape[3]
    slabs = point_damping.shape[0] // slab_len
    cam_dev = right_side.shape[1]
    rows = cam_dev // LANES
    owners = lax.axis_size("pt")
    parts = lax.axis_size("cam")
    part_len = slab_len // parts
    lists = (block_ids.reshape(pairs), slab_ids.reshape(pairs), pair_count.reshape(1))
    idx = cam_index.reshape(pairs, slab_len)
    jc = cam_jacobian.reshape(pairs, 18, slab_len).transpose(1, 0, 2)
    jp = point_jacobian.reshape(pairs, 6, slab_len).transpose(1, 0, 2)
    residual = right_side.reshape(9, rows, LANES)
    damping = cam_damping.reshape(9, rows, LANES)
    part = lax.axis_index("cam")
    point_damp = lax.dynamic_slice_in_dim(
        point_damping.reshape(slabs, slab_len), part * part_len, part_len, 1
    )
    direction = residual
    answer = jnp.zeros_like(residual)
    cams = swap(direction, "pt", True, 0)
    norm_group = jnp.sum(cams * cams)
    norm_now = None
    inverse = None
    for iteration in range(ITERS):
        if iteration == 0:
            y, proj = forward(True, lists, cams, idx, jc, jp, parts, slabs)
            merged = swap(y, "cam", False, 1)
            pulled = merged[:3]
            inverse = invert_points(merged[3:], point_damp)
        else:
            y, proj = forward(False, lists, cams, idx, jc, jp, parts, slabs)
            pulled = swap(y, "cam", False, 2)
        z = swap(apply_inverse(inverse, pulled), "cam", True, 3)
        sums = backward(lists, z, proj, idx, jc, jp, owners, rows)
        image = damping * direction + swap(sums, "pt", False, 4)
        curve = over_pt(jnp.sum(direction * image))
        if iteration == 0:
            both = over_cam([curve, norm_group])
            curve, norm_now = both[0], both[1]
        else:
            curve = over_cam([curve])[0]
        step_size = norm_now / curve
        answer = answer + step_size * direction
        residual = residual - step_size * image
        if iteration + 1 < ITERS:
            group = swap(residual, "pt", True, 0)
            norm_next = over_cam([jnp.sum(group * group)])[0]
            ratio = norm_next / norm_now
            cams = group + ratio * cams
            direction = residual + ratio * direction
            norm_now = norm_next
    return answer.reshape(9, cam_dev), residual.reshape(9, cam_dev)


def solution(mesh):
    in_specs = (
        P(None, ("cam", "pt")),
        P(None, ("cam", "pt")),
        P("pt"),
        P("cam", "pt", None),
        P("cam", "pt", None),
        P("cam", "pt", None, None),
        P("cam", "pt", None, None, None),
        P("cam", "pt", None, None, None),
        P("cam", "pt"),
    )
    out_specs = (P(None, ("cam", "pt")), P(None, ("cam", "pt")))
    return jax.shard_map(
        per_device, mesh=mesh, in_specs=in_specs, out_specs=out_specs, check_vma=False
    )
```

profile of v0, /device:TPU:0, one launch (start us, length us, event | category | flops | bytes accessed | tf_op | source)
XLA Modules:
  0.0 267.1 jit_solution(7309747578162263697)
XLA Ops:
  0.6 0.9 copy.11
  1.6 15.6 %gather_pt.4.cam_ref = f32[8,9,16,128]{3,2,1,0:T(8,128)S(1)} custom-call(f32[9,16,128]{2,1,0:T(8,128)S(1)} %slice.107.x_ref), custom_call_target="tpu_custom_call" | custom-call | tf_op jit(solution)/shard_map/gather_pt/pallas_call | solution.py:303
  17.2 0.8 copy-done
  18.7 12.9 %forward_first.1 = (f32[4,9,16,1024]{3,2,1,0:T(8,128)}, f32[2,64,4096]{2,1,0:T(8,128)}) custom-call(s32[64]{0:T(128)} %bitcast.227, s32[64]{0:T(128)} %bitcast.231, s32[1]{0:T(128)} %bitcast.196.count, f32[8,9,16,128]{3,2,1,0:T(8,128)} %copy-done, s32[64,4096]{1,0:T(8,128)} %bitcast.208, bf16[18,64,4096]{2,1,0:T(8,128)(2,1)} %bitcast.200, ...), custom_call_target="tpu_custom_call" | custom-call | tf_op jit(solution)/shard_map/forward_first/pallas_call | solution.py:214
  31.6 1.7 copy-done.6
  33.3 30.1 %scatter_cam.2 = f32[9,16,1024]{2,1,0:T(8,128)S(1)} custom-call(f32[4,9,16,1024]{3,2,1,0:T(8,128)S(1)} %copy-done.6), custom_call_target="tpu_custom_call" | custom-call | tf_op jit(solution)/shard_map/scatter_cam/pallas_call | solution.py:303
  63.5 0.1 fusion.10
  63.5 0.1 fusion.12
  63.7 11.0 %gather_cam.5.z_ref = f32[4,3,16,1024]{3,2,1,0:T(8,128)S(1)} custom-call(f32[3,16,1024]{2,1,0:T(8,128)S(1)} %pad_maximum_fusion.x_ref), custom_call_target="tpu_custom_call" | custom-call | tf_op jit(solution)/shard_map/gather_cam/pallas_call | solution.py:303
  74.7 0.9 copy-done.3
  75.5 15.7 %backward.2.x_ref = f32[8,9,16,128]{3,2,1,0:T(8,128)} custom-call(s32[64]{0:T(128)} %bitcast.228, s32[64]{0:T(128)} %bitcast.232, s32[1]{0:T(128)} %bitcast.197.count, f32[4,3,16,1024]{3,2,1,0:T(8,128)} %copy-done.3, f32[2,64,4096]{2,1,0:T(8,128)} %get-tuple-element.7.proj_ref, s32[64,4096]{1,0:T(8,128)} %bitcast.209, bf16[18,64,4096]{2,1,0:T(8,128)(2,1)} %bitcast.201, ...), custom_call_target="tpu_custom_call" | custom-call | tf_op jit(solution)/shard_map/backward/pallas_call | solution.py:236
  91.2 1.1 copy-done.5
  92.3 28.2 %scatter_pt.2 = f32[9,16,128]{2,1,0:T(8,128)S(1)} custom-call(f32[8,9,16,128]{3,2,1,0:T(8,128)S(1)} %copy-done.5), custom_call_target="tpu_custom_call" | custom-call | tf_op jit(solution)/shard_map/scatter_pt/pallas_call | solution.py:303
  120.5 0.6 multiply_reduce_fusion.3
  121.2 0.6 broadcast_in_dim.10.x_ref
  121.8 10.8 %gather_pt.5 = f32[8,1,8,128]{3,2,1,0:T(8,128)S(1)} custom-call(f32[1,8,128]{2,1,0:T(8,128)S(1)} %broadcast_in_dim.10.x_ref), custom_call_target="tpu_custom_call" | custom-call | tf_op jit(solution)/shard_map/gather_pt/pallas_call | solution.py:303
  132.6 0.7 slice_reduce_fusion.4
  133.3 0.7 multiply_reduce_fusion.1
  134.0 1.4 pad_maximum_fusion.4
  135.4 0.1 broadcast_in_dim.11.x_ref
  135.5 5.4 %gather_cam.6 = f32[4,2,8,128]{3,2,1,0:T(8,128)S(1)} custom-call(f32[2,8,128]{2,1,0:T(8,128)S(1)} %broadcast_in_dim.11.x_ref), custom_call_target="tpu_custom_call" | custom-call | tf_op jit(solution)/shard_map/gather_cam/pallas_call | solution.py:303
  140.9 0.1 slice_reduce_fusion.3
  141.0 0.7 fusion.35
  143.0 14.1 %gather_pt.6 = f32[8,9,16,128]{3,2,1,0:T(8,128)S(1)} custom-call(f32[9,16,128]{2,1,0:T(8,128)S(1)} %multiply_subtract_fusion.1.x_ref), custom_call_target="tpu_custom_call" | custom-call | tf_op jit(solution)/shard_map/gather_pt/pallas_call | solution.py:303
  157.1 0.7 multiply_reduce_fusion
  157.9 0.6 pad_maximum_fusion.3
  158.5 0.1 broadcast_in_dim.12.x_ref
  158.6 3.7 %gather_cam.7 = f32[4,2,8,128]{3,2,1,0:T(8,128)S(1)} custom-call(f32[2,8,128]{2,1,0:T(8,128)S(1)} %broadcast_in_dim.12.x_ref), custom_call_target="tpu_custom_call" | custom-call | tf_op jit(solution)/shard_map/gather_cam/pallas_call | solution.py:303
  162.3 0.1 slice_reduce_fusion.2
  163.2 0.9 multiply_add_fusion.cam_ref
  164.1 11.4 %forward_next.1 = (f32[4,3,16,1024]{3,2,1,0:T(8,128)}, f32[2,64,4096]{2,1,0:T(8,128)}) custom-call(s32[64]{0:T(128)} %bitcast.229, s32[64]{0:T(128)} %bitcast.233, s32[1]{0:T(128)} %bitcast.198.count, f32[8,9,16,128]{3,2,1,0:T(8,128)} %multiply_add_fusion.cam_ref, s32[64,4096]{1,0:T(8,128)} %bitcast.210, bf16[18,64,4096]{2,1,0:T(8,128)(2,1)} %bitcast.202, ...), custom_call_target="tpu_custom_call" | custom-call | tf_op jit(solution)/shard_map/forward_next/pallas_call | solution.py:214
  175.5 1.1 copy-done.7
  176.6 13.4 %scatter_cam.3 = f32[3,16,1024]{2,1,0:T(8,128)S(1)} custom-call(f32[4,3,16,1024]{3,2,1,0:T(8,128)S(1)} %copy-done.7), custom_call_target="tpu_custom_call" | custom-call | tf_op jit(solution)/shard_map/scatter_cam/pallas_call | solution.py:303
  190.1 11.0 %gather_cam.8.z_ref = f32[4,3,16,1024]{3,2,1,0:T(8,128)S(1)} custom-call(f32[3,16,1024]{2,1,0:T(8,128)S(1)} %pad_maximum_fusion.1.x_ref), custom_call_target="tpu_custom_call" | custom-call | tf_op jit(solution)/shard_map/gather_cam/pallas_call | solution.py:303
  201.1 0.9 copy-done.2
  202.0 15.6 %backward.3.x_ref = f32[8,9,16,128]{3,2,1,0:T(8,128)} custom-call(s32[64]{0:T(128)} %bitcast.230, s32[64]{0:T(128)} %bitcast.234, s32[1]{0:T(128)} %bitcast.199.count, f32[4,3,16,1024]{3,2,1,0:T(8,128)} %copy-done.2, f32[2,64,4096]{2,1,0:T(8,128)} %get-tuple-element.9.proj_ref, s32[64,4096]{1,0:T(8,128)} %bitcast.211, bf16[18,64,4096]{2,1,0:T(8,128)(2,1)} %bitcast.203, ...), custom_call_target="tpu_custom_call" | custom-call | tf_op jit(solution)/shard_map/backward/pallas_call | solution.py:236
  217.6 1.1 copy-done.4
  218.6 26.2 %scatter_pt.3 = f32[9,16,128]{2,1,0:T(8,128)S(1)} custom-call(f32[8,9,16,128]{3,2,1,0:T(8,128)S(1)} %copy-done.4), custom_call_target="tpu_custom_call" | custom-call | tf_op jit(solution)/shard_map/scatter_pt/pallas_call | solution.py:303
  244.8 0.6 multiply_reduce_fusion.2
  245.4 0.6 broadcast_in_dim.13.x_ref
  246.1 11.5 %gather_pt.7 = f32[8,1,8,128]{3,2,1,0:T(8,128)S(1)} custom-call(f32[1,8,128]{2,1,0:T(8,128)S(1)} %broadcast_in_dim.13.x_ref), custom_call_target="tpu_custom_call" | custom-call | tf_op jit(solution)/shard_map/gather_pt/pallas_call | solution.py:303
  257.6 0.6 slice_reduce_fusion.1
  258.2 0.7 pad_maximum_fusion.2
  258.9 0.1 broadcast_in_dim.14.x_ref
  259.0 6.4 %gather_cam.9 = f32[4,2,8,128]{3,2,1,0:T(8,128)S(1)} custom-call(f32[2,8,128]{2,1,0:T(8,128)S(1)} %broadcast_in_dim.14.x_ref), custom_call_target="tpu_custom_call" | custom-call | tf_op jit(solution)/shard_map/gather_cam/pallas_call | solution.py:303
  265.4 0.1 slice_reduce_fusion
  265.6 0.7 copy.13
  266.4 0.7 copy.14
  (25 shorter events, 0.3 us)
Async XLA Ops:
  17.2 0.8 copy-start
  31.6 1.7 copy-start.6
  33.3 30.1 %copy-start.8 = (f32[65536]{0:T(1024)S(1)}, f32[65536]{0:T(1024)}, u32[]{:S(2)}) copy-start(f32[65536]{0:T(1024)} %param.11) | copy-start | bytes 786436
  74.7 0.9 copy-start.3
  75.5 45.0 %copy-start.9 = (f32[9,2048]{1,0:T(8,128)S(1)}, f32[9,2048]{1,0:T(8,128)}, u32[]{:S(2)}) copy-start(f32[9,2048]{1,0:T(8,128)} %param.10) | copy-start | bytes 221188
  75.5 57.7 %copy-start.1 = (f32[8,9,16,128]{3,2,1,0:T(8,128)S(1)}, f32[8,9,16,128]{3,2,1,0:T(8,128)}, u32[]{:S(2)}) copy-start(f32[8,9,16,128]{3,2,1,0:T(8,128)} %copy-done) | copy-start | bytes 1769476
  91.2 1.1 copy-start.5
  175.5 1.1 copy-start.7
  201.1 0.9 copy-start.2
  217.6 1.1 copy-start.4
where the time goes:
time: 269 us; the launch traced here: 267 us
  Pallas kernels  243 us (90%)
  local copies, waits for them, and re-layouts  12.1 us (4%)
  other arithmetic  8.33 us (3%)
  between operations  3.79 us (1%)
    pallas_call x13, Pallas kernels, swap(): pl.pallas_call(functools.partial(swap_kernel, axis, gather), name=('gathe...  187 us
    pallas_call x2, Pallas kernels, backward(): pl.pallas_call(backward_kernel, name='backward', out_shape=jax.ShapeDtype...  31.3 us
    pallas_call x2, Pallas kernels, forward(): pl.pallas_call(functools.partial(forward_kernel, first), name='forward_fi...  24.3 us
    unnamed x26, local copies, waits for them, and re-layouts  9.89 us

commit v1 on v0

v1 whole, which is shorter than its diff:
```python
import functools

import jax
import jax.numpy as jnp
from jax import lax
from jax.experimental import pallas as pl
from jax.experimental.pallas import tpu as pltpu
from jax.sharding import PartitionSpec as P

BLOCK = 64
ITERS = 2
LANES = 128
CHUNKS = 4
COLS = 5 * LANES
F32 = jnp.float32
BF16 = jnp.bfloat16
VMEM_BYTES = 60 * 1024 * 1024
MESH = pl.DeviceIdType.MESH
HESS = [(0, 0), (1, 1), (2, 2), (0, 1), (1, 2), (0, 2)]


def iota(shape, axis):
    return lax.broadcasted_iota(jnp.int32, shape, axis)


def split2(value):
    high = value.astype(BF16)
    return high, (value - high.astype(F32)).astype(BF16)


def split3(value):
    high, low = split2(value)
    last = value - high.astype(F32) - low.astype(F32)
    return high, low, last.astype(BF16)


def dot(a, b):
    return jnp.dot(a, b, preferred_element_type=F32)


def select_rows(hot, value):
    parts = split3(value)
    return dot(hot, parts[0]) + dot(hot, parts[1]) + dot(hot, parts[2])


def invert(hess, damping):
    xx, yy, zz = (hess[k] + damping for k in range(3))
    xy, yz, xz = hess[3], hess[4], hess[5]
    cof_xx = yy * zz - yz * yz
    cof_xy = xz * yz - xy * zz
    cof_xz = xy * yz - xz * yy
    cof_yy = xx * zz - xz * xz
    cof_yz = xy * xz - xx * yz
    cof_zz = xx * yy - xy * xy
    det = xx * cof_xx + xy * cof_xy + xz * cof_xz
    return [c / det for c in (cof_xx, cof_xy, cof_xz, cof_yy, cof_yz, cof_zz)]


def apply_inverse(inv, vec):
    return [
        inv[0] * vec[0] + inv[1] * vec[1] + inv[2] * vec[2],
        inv[1] * vec[0] + inv[3] * vec[1] + inv[4] * vec[2],
        inv[2] * vec[0] + inv[4] * vec[1] + inv[5] * vec[2],
    ]


def body(
    ids_ref, slab_ref, count_ref, rs_ref, damp_ref, pdamp_ref, idx_hbm, jc_hbm, jp_hbm,
    answer_ref, residual_ref,
    idx, jc, jp, load_sem,
    place, place_t, pick, pick_t, sums_by_slab, slab_hot_t, asks_mine, asks,
    flat, v0, v1, v2, damp, packed, got, tables, proj, tbuf, zslot, pbuf, acc, slotsum,
    h_part, h_sib, h_red, h_far, inverse, y_part, y_sib, y_red, y_far, z_all,
    out_pack, in_pack, dots, dots_pt, dots_cam,
    ask_send, ask_recv, a_send, a_recv, e_send, e_recv,
    hs_sem, hx_sem, ys_sem, yx_sem, zx_sem, zs_sem, dp_sem, dc_sem,
):
    pairs, points = idx.shape
    owners = lax.axis_size("pt")
    ncam = lax.axis_size("cam")
    nx = ncam // 2
    me_pt = lax.axis_index("pt")
    me_cam = lax.axis_index("cam")
    me_x = me_cam // 2
    me_core = lax.rem(me_cam, 2)
    sibling = me_x * 2 + (1 - me_core)
    spots = 2 * pairs
    cap = spots // owners
    slabs = sums_by_slab.shape[0]
    width = points // CHUNKS
    part = width // ncam
    half = v0.shape[0] // 2
    row_tiles = points // LANES

    def far(hop):
        return lax.rem(me_x + hop, nx)

    def at_cam(cam):
        return {"cam": cam}

    def at_pt(pt):
        return {"pt": pt}

    loads = [
        pltpu.make_async_copy(jp_hbm, jp, load_sem.at[0]),
        pltpu.make_async_copy(idx_hbm, idx, load_sem.at[1]),
        pltpu.make_async_copy(jc_hbm, jc, load_sem.at[2]),
    ]
    for copy in loads:
        copy.start()

    barrier = pltpu.get_barrier_semaphore()
    for hop in range(1, owners):
        pl.semaphore_signal(
            barrier, inc=1, device_id=at_pt(lax.rem(me_pt + hop, owners)), device_id_type=MESH
        )
    for hop in range(1, ncam):
        pl.semaphore_signal(
            barrier, inc=1, device_id=at_cam(lax.rem(me_cam + hop, ncam)), device_id_type=MESH
        )

    square = (LANES, LANES)
    sub, lane = iota(square, 0), iota(square, 1)
    blank = jnp.zeros((1, LANES - pairs), F32)
    ids_row = jnp.concatenate([ids_ref[...].astype(F32), blank], axis=1)
    slab_row = jnp.concatenate([slab_ref[...].astype(F32), blank], axis=1)
    count = jnp.broadcast_to(count_ref[...], square)
    live_row = lane < count
    live_col = sub < count
    ids_row = jnp.broadcast_to(ids_row, square).astype(jnp.int32)
    slab_row = jnp.broadcast_to(slab_row, square)
    ids_col = ids_row.astype(F32).T.astype(jnp.int32)
    blocks_dev = 2 * half
    owner_row = ids_row // blocks_dev
    owner_col = ids_col // blocks_dev
    same = jnp.where(owner_row == owner_col, 1.0, 0.0)
    before = jnp.where((lane < sub) & live_row, same, 0.0)
    rank_col = jnp.broadcast_to(jnp.sum(before, axis=1, keepdims=True), square)
    pos_col = owner_col * cap + rank_col.astype(jnp.int32)
    pos_row = pos_col.astype(F32).T.astype(jnp.int32)
    pick_f = jnp.where((pos_row == sub) & live_row, 1.0, 0.0)
    pick_tf = jnp.where((pos_col == lane) & live_col, 1.0, 0.0)
    local = ids_row - owner_row * blocks_dev
    local = local // 2 + half * (local - (local // 2) * 2)
    asked = jnp.sum(pick_f * (local + 1).astype(F32), axis=1, keepdims=True) - 1.0
    asks_mine[...] = jnp.broadcast_to(asked, square).reshape(owners, cap, LANES)
    pick[:, :pairs] = pick_f[:, :pairs].astype(BF16)
    pick[:, pairs:] = pick_f[:, :pairs].astype(BF16)
    pick_t[...] = pick_tf[:pairs, :].astype(BF16)
    hot_slab = jnp.where((slab_row == sub.astype(F32)) & live_row, 1.0, 0.0)
    hot_slab_t = hot_slab.T
    sums_by_slab[:, :pairs] = hot_slab[:slabs, :pairs].astype(BF16)
    sums_by_slab[:, pairs:] = hot_slab[:slabs, :pairs].astype(BF16)
    slab_hot_t[:, :slabs] = hot_slab_t[:pairs, :slabs].astype(BF16)
    slab_hot_t[:, slabs:] = hot_slab_t[:pairs, :slabs].astype(BF16)

    wide = (half, LANES)
    low_lane = iota(wide, 1) < BLOCK

    def to_rows(source, target):
        for r in range(half):
            cols = pl.ds(r * LANES, LANES)
            flat[pl.ds(r, 8, stride=half), :] = source[0:8, cols]
            flat[8 * half + r : 8 * half + r + 1, :] = source[8:9, cols]
        for i in range(5):
            left = flat[pl.ds(2 * i * half, half), :]
            if i < 4:
                right = flat[pl.ds((2 * i + 1) * half, half), :]
            else:
                right = jnp.zeros(wide, F32)
            cols = pl.ds(i * LANES, LANES)
            target[0:half, cols] = jnp.where(low_lane, left, pltpu.roll(right, BLOCK, 1))
            target[half:, cols] = jnp.where(low_lane, pltpu.roll(left, BLOCK, 1), right)

    def from_rows(value, target):
        for i in range(5):
            even = value[0:half, i * LANES : (i + 1) * LANES]
            odd = value[half:, i * LANES : (i + 1) * LANES]
            flat[pl.ds(2 * i * half, half), :] = jnp.where(low_lane, even, pltpu.roll(odd, BLOCK, 1))
            if i < 4:
                flat[pl.ds((2 * i + 1) * half, half), :] = jnp.where(
                    low_lane, pltpu.roll(even, BLOCK, 1), odd
                )
        for r in range(half):
            cols = pl.ds(r * LANES, LANES)
            target[0:8, cols] = flat[pl.ds(r, 8, stride=half), :]
            target[8:9, cols] = flat[8 * half + r : 8 * half + r + 1, :]

    to_rows(rs_ref, v0)
    to_rows(damp_ref, damp)

    pl.semaphore_wait(barrier, owners + ncam - 2)

    def pt_exchange(sources, target, send_sem, recv_sem):
        copies = []
        for hop in range(1, owners):
            peer = lax.rem(me_pt + hop, owners)
            copy = pltpu.make_async_remote_copy(
                src_ref=sources(peer), dst_ref=target.at[me_pt],
                send_sem=send_sem.at[hop - 1], recv_sem=recv_sem.at[hop - 1],
                device_id=at_pt(peer), device_id_type=MESH,
            )
            copy.start()
            copies.append(copy)
        return copies

    def wait_all(copies):
        for copy in copies:
            copy.wait()

    ask_copies = pt_exchange(lambda peer: asks_mine.at[peer], asks, ask_send, ask_recv)
    asks[me_pt] = asks_mine[me_pt]

    def to_sibling(source, target, sems, c):
        copy = pltpu.make_async_remote_copy(
            src_ref=source, dst_ref=target, send_sem=sems.at[0, c], recv_sem=sems.at[1, c],
            device_id=at_cam(sibling), device_id_type=MESH,
        )
        copy.start()
        return [copy]

    def to_far(source, target, sems, c):
        copies = []
        for hop in range(1, nx):
            peer = far(hop)
            copy = pltpu.make_async_remote_copy(
                src_ref=source(peer), dst_ref=target(hop),
                send_sem=sems.at[0, c, hop - 1], recv_sem=sems.at[1, c, hop - 1],
                device_id=at_cam(peer * 2 + me_core), device_id_type=MESH,
            )
            copy.start()
            copies.append(copy)
        return copies

    def put_parts(buf, c, k, value):
        for q in range(ncam):
            buf[c, q % 2, q // 2, k] = value[:, q * part : (q + 1) * part]

    loads[0].wait()
    h_copies = []
    for c in range(CHUNKS):

        def hess_tile(t, carry, c=c):
            col = pl.multiple_of(c * width + t * LANES, LANES)
            spot = pl.ds(pl.multiple_of(t * LANES, LANES), LANES)
            for g in range(pairs // 16):
                rows = slice(g * 16, g * 16 + 16)
                point = [jp[k, rows, pl.ds(col, LANES)].astype(F32) for k in range(6)]
                for f, (a, b) in enumerate(HESS):
                    high, low = split2(point[a] * point[b] + point[3 + a] * point[3 + b])
                    tbuf[f, rows, spot] = high
                    tbuf[f, pairs + g * 16 : pairs + g * 16 + 16, spot] = low
            return carry

        lax.fori_loop(0, width // LANES, hess_tile, 0)
        for f in range(6):
            put_parts(h_part, c, f, dot(sums_by_slab[...], tbuf[f]))
        h_copies.append(to_sibling(h_part.at[c, 1 - me_core], h_sib.at[c], hs_sem, c))

    wait_all(ask_copies)
    wanted = asks[...].reshape(spots, LANES)
    hot = jnp.where(wanted == lane.astype(F32), 1.0, 0.0)
    place[...] = hot[:, : 2 * half].astype(BF16)
    place_t[...] = hot.T[: 2 * half, :].astype(BF16)

    def send_blocks(vec, it):
        out = select_rows(place[...], vec[...])
        packed[it] = out.reshape(owners, cap, COLS)
        got[it, me_pt] = packed[it, me_pt]
        return pt_exchange(
            lambda peer: packed.at[it, peer], got.at[it], a_send.at[it], a_recv.at[it]
        )

    def make_tables(it):
        value = select_rows(pick_t[...], got[it].reshape(spots, COLS))
        for i in range(5):
            tables[i] = value[:, i * LANES : (i + 1) * LANES]

    a_copies = send_blocks(v0, 0)

    h_far_copies = []
    for c in range(CHUNKS):
        wait_all(h_copies[c])
        h_red[c] = h_part[c, me_core] + h_sib[c]
        h_far_copies.append(
            to_far(lambda peer: h_red.at[c, peer], lambda hop: h_far.at[c, hop - 1], hx_sem, c)
        )

    def finish_hessian(c):
        wait_all(h_far_copies[c])
        for t in range(part // LANES):
            cols = pl.ds(t * LANES, LANES)
            hess = []
            for f in range(6):
                total = h_red[c, me_x, f, :, cols]
                for hop in range(1, nx):
                    total = total + h_far[c, hop - 1, f, :, cols]
                hess.append(total)
            tile = (c * width + me_cam * part) // LANES + t
            damping = pdamp_ref[pl.ds(tile, slabs, stride=row_tiles), :]
            for f, value in enumerate(invert(hess, damping)):
                inverse[c, f, :, cols] = value

    def forward(c, it):
        def tile(t, carry):
            col = pl.multiple_of(c * width + t * LANES, LANES)
            cols = pl.ds(col, LANES)
            spot = pl.ds(pl.multiple_of(t * LANES, LANES), LANES)
            for g in range(pairs // 16):
                rows = slice(g * 16, g * 16 + 16)
                index = [idx[rows, cols]]
                index.append(index[0] + BLOCK)
                pr = [None, None]
                for k in range(9):
                    at_camera = jnp.take_along_axis(
                        tables[k // 2, rows, :], index[k % 2], axis=1, mode="promise_in_bounds"
                    )
                    for i in range(2):
                        term = jc[9 * i + k, rows, cols].astype(F32) * at_camera
                        pr[i] = term if k == 0 else pr[i] + term
                for i in range(2):
                    proj[i, rows, cols] = pr[i]
                for f in range(3):
                    made = (
                        jp[f, rows, cols].astype(F32) * pr[0]
                        + jp[3 + f, rows, cols].astype(F32) * pr[1]
                    )
                    high, low = split2(made)
                    tbuf[f, rows, spot] = high
                    tbuf[f, pairs + g * 16 : pairs + g * 16 + 16, spot] = low
            return carry

        lax.fori_loop(0, width // LANES, tile, 0)
        for f in range(3):
            put_parts(y_part.at[it], c, f, dot(sums_by_slab[...], tbuf[f]))
        return to_sibling(
            y_part.at[it, c, 1 - me_core], y_sib.at[it, c], ys_sem.at[it], c
        )

    def reduce_sibling(c, it, copies):
        wait_all(copies)
        y_red[it, c] = y_part[it, c, me_core] + y_sib[it, c]
        return to_far(
            lambda peer: y_red.at[it, c, peer],
            lambda hop: y_far.at[it, c, hop - 1],
            yx_sem.at[it], c,
        )

    def eliminate(c, it, copies):
        if it == 0:
            finish_hessian(c)
        wait_all(copies)
        vec = []
        for f in range(3):
            total = y_red[it, c, me_x, f]
            for hop in range(1, nx):
                total = total + y_far[it, c, hop - 1, f]
            vec.append(total)
        for f, value in enumerate(apply_inverse([inverse[c, f] for f in range(6)], vec)):
            z_all[it, c, me_core, me_x, f] = value
        here = z_all.at[it, c, me_core, me_x]
        return to_far(lambda peer: here, lambda hop: here, zx_sem.at[it], c)

    def share(c, it, copies):
        wait_all(copies)
        here = z_all.at[it, c, me_core]
        return to_sibling(here, here, zs_sem.at[it], c)

    def backward(c, it, copies):
        wait_all(copies)
        for q in range(ncam):
            for f in range(3):
                high, low = split2(z_all[it, c, q % 2, q // 2, f])
                zslot[f, :, q * part : (q + 1) * part] = dot(
                    slab_hot_t[...], jnp.concatenate([high, low], axis=0)
                )

        def group(g, carry):
            base = pl.multiple_of(g * 16, 16)
            rows = pl.ds(base, 16)
            for t in range(width // LANES):
                cols = pl.ds(c * width + t * LANES, LANES)
                spot = pl.ds(t * LANES, LANES)
                miss = [proj[i, rows, cols] for i in range(2)]
                for f in range(3):
                    z = zslot[f, rows, spot]
                    for i in range(2):
                        miss[i] = miss[i] - jp[3 * i + f, rows, cols].astype(F32) * z
                push = [
                    jc[k, rows, cols].astype(F32) * miss[0]
                    + jc[9 + k, rows, cols].astype(F32) * miss[1]
                    for k in range(9)
                ]
                for h in range(2):
                    mine = [value[h * 8 : h * 8 + 8] for value in push]
                    last_high = mine[8].astype(BF16).astype(F32)
                    for i in range(4):
                        pair = jnp.concatenate([mine[2 * i], mine[2 * i + 1]], axis=0)
                        high, low = split2(pair)
                        pbuf[h, 16 * i : 16 * i + 16, spot] = high
                        pbuf[h, 80 + 16 * i : 96 + 16 * i, spot] = low
                    pair = jnp.concatenate([last_high, mine[8] - last_high], axis=0)
                    pbuf[h, 64:80, spot] = pair.astype(BF16)
            cams = iota((BLOCK, 2 * LANES), 0)
            for h in range(2):
                for s in range(2):
                    total = None
                    for t in range(width // (2 * LANES)):
                        cols = pl.ds(c * width + t * 2 * LANES, 2 * LANES)
                        here = idx[pl.ds(pl.multiple_of(base + h * 8, 8), 8), cols]
                        hots = []
                        for j in range(4):
                            line = here[s * 4 + j : s * 4 + j + 1, :]
                            line = jnp.broadcast_to(line, (BLOCK, 2 * LANES))
                            hots.append(jnp.where(cams == line, 1.0, 0.0).astype(BF16))
                        piece = lax.dot_general(
                            pbuf[h, :, t * 2 * LANES : (t + 1) * 2 * LANES],
                            jnp.concatenate(hots, axis=0),
                            (((1,), (1,)), ((), ())),
                            preferred_element_type=F32,
                        )
                        total = piece if total is None else total + piece
                    if c == 0:
                        acc[2 * g + h, s] = total
                    else:
                        acc[2 * g + h, s] += total
            return carry

        lax.fori_loop(0, pairs // 16, group, 0)

    def slot_sums():
        small = (8, LANES)
        row = iota(small, 0)
        first4 = row < 4
        right = lax.rem(row, 4) >= 2
        odd = lax.rem(row, 2) == 1
        low8 = iota(small, 1) < BLOCK

        def one(g, carry):
            lows, highs = [], []
            for f in range(9):
                other = 72 if f == 8 else 80 + 8 * f
                cut = []
                for s in range(2):
                    cut.append(acc[g, s, 8 * f : 8 * f + 8, :] + acc[g, s, other : other + 8, :])
                here = jnp.where(
                    right,
                    jnp.where(first4, cut[0][:, LANES:], cut[1][:, LANES:]),
                    jnp.where(first4, cut[0][:, :LANES], cut[1][:, :LANES]),
                )
                turned = pltpu.roll(here, BLOCK, 1)
                lows.append(jnp.where(odd, turned, here))
                highs.append(jnp.where(odd, here, turned))
            rows = pl.ds(pl.multiple_of(g * 8, 8), 8)
            for i in range(5):
                high = highs[2 * i + 1] if i < 4 else jnp.zeros(small, F32)
                slotsum[rows, i * LANES : (i + 1) * LANES] = jnp.where(low8, lows[2 * i], high)
            return carry

        lax.fori_loop(0, pairs // 8, one, 0)

    def schur(vec, it, a_copies, beside):
        wait_all(a_copies)
        make_tables(it)
        next(beside, None)
        if it == 0:
            loads[1].wait()
            loads[2].wait()
        first, second, third, fourth = {}, {}, {}, {}
        for step in range(CHUNKS + 3):
            if step < CHUNKS:
                first[step] = forward(step, it)
                next(beside, None)
            if 0 <= step - 1 < CHUNKS:
                second[step - 1] = reduce_sibling(step - 1, it, first[step - 1])
            if 0 <= step - 2 < CHUNKS:
                third[step - 2] = eliminate(step - 2, it, second[step - 2])
            if 0 <= step - 3 < CHUNKS:
                fourth[step - 3] = share(step - 3, it, third[step - 3])
            if step - 3 >= 0 and step >= CHUNKS - 1:
                backward(step - 3, it, fourth[step - 3])
        slot_sums()
        next(beside, None)
        high, low = split2(slotsum[...])
        out = dot(pick[...], jnp.concatenate([high, low], axis=0))
        out_pack[it] = out.reshape(owners, cap, COLS)
        in_pack[it, me_pt] = out_pack[it, me_pt]
        copies = pt_exchange(
            lambda peer: out_pack.at[it, peer], in_pack.at[it], e_send.at[it], e_recv.at[it]
        )
        wait_all(copies)
        high, low = split2(in_pack[it].reshape(spots, COLS))
        total = dot(place_t[...], high) + dot(place_t[...], low)
        return damp[...] * vec[...] + total

    def fill(value):
        return jnp.broadcast_to(jnp.sum(value, keepdims=True), (8, LANES))

    def start_dots(values, n):
        for k, value in enumerate(values):
            dots[n, k] = fill(value)
        copies = []
        for hop in range(1, owners):
            copy = pltpu.make_async_remote_copy(
                src_ref=dots.at[n], dst_ref=dots_pt.at[n, hop - 1],
                send_sem=dp_sem.at[0, n, hop - 1], recv_sem=dp_sem.at[1, n, hop - 1],
                device_id=at_pt(lax.rem(me_pt + hop, owners)), device_id_type=MESH,
            )
            copy.start()
            copies.append(copy)
        return copies

    def pass_dots(copies, n):
        wait_all(copies)
        total = dots[n]
        for hop in range(1, owners):
            total = total + dots_pt[n, hop - 1]
        dots_cam[n, 0] = total
        copies = []
        for hop in range(1, ncam):
            copy = pltpu.make_async_remote_copy(
                src_ref=dots_cam.at[n, 0], dst_ref=dots_cam.at[n, hop],
                send_sem=dc_sem.at[0, n, hop - 1], recv_sem=dc_sem.at[1, n, hop - 1],
                device_id=at_cam(lax.rem(me_cam + hop, ncam)), device_id_type=MESH,
            )
            copy.start()
            copies.append(copy)
        return copies

    def end_dots(copies, n, k):
        wait_all(copies)
        total = dots_cam[n, 0]
        for hop in range(1, ncam):
            total = total + dots_cam[n, hop]
        return [total[i][0:1, 0:1] for i in range(k)]

    v1[...] = schur(v0, 0, a_copies, iter(()))
    a_copies = send_blocks(v1, 1)
    known = []

    def scalars(copies):
        copies = pass_dots(copies, 0)
        yield
        yield
        norm0, curve0 = end_dots(copies, 0, 2)
        step0 = norm0 / curve0
        res1 = v0[...] - step0 * v1[...]
        copies = start_dots([res1 * res1], 1)
        yield
        yield
        copies = pass_dots(copies, 1)
        yield
        (norm1,) = end_dots(copies, 1, 1)
        known.extend([norm0, norm1, step0])
        yield

    copies = start_dots([v0[...] * v0[...], v0[...] * v1[...]], 0)
    v2[...] = schur(v1, 1, a_copies, scalars(copies))
    norm0, norm1, step0 = known
    res1 = v0[...] - step0 * v1[...]
    ratio = norm1 / norm0
    dir1 = res1 + ratio * v0[...]
    image1 = v1[...] - step0 * v2[...] + ratio * v1[...]
    three = start_dots([dir1 * image1], 2)
    three = pass_dots(three, 2)
    (curve1,) = end_dots(three, 2, 1)
    step1 = norm1 / curve1
    from_rows(step0 * v0[...] + step1 * dir1, answer_ref)
    from_rows(res1 - step1 * image1, residual_ref)


def per_device(
    right_side, cam_damping, point_damping, block_ids, slab_ids, cam_index, cam_jacobian,
    point_jacobian, pair_count,
):
    pairs = block_ids.shape[2]
    points = cam_index.shape[3]
    slabs = point_damping.shape[0] // points
    cam_dev = right_side.shape[1]
    blocks_dev = cam_dev // BLOCK
    owners = lax.axis_size("pt")
    ncam = lax.axis_size("cam")
    nx = ncam // 2
    spots = 2 * pairs
    cap = spots // owners
    width = points // CHUNKS
    part = width // ncam
    idx = cam_index.reshape(pairs, points)
    jc = cam_jacobian.reshape(pairs, 18, points).transpose(1, 0, 2)
    jp = point_jacobian.reshape(pairs, 6, points).transpose(1, 0, 2)
    vmem = pl.BlockSpec(memory_space=pltpu.VMEM)
    hbm = pl.BlockSpec(memory_space=pl.ANY)
    V = pltpu.VMEM
    D = pltpu.SemaphoreType.DMA
    far = max(nx - 1, 1)
    scratch = [
        V((pairs, points), jnp.int32), V((18, pairs, points), BF16), V((6, pairs, points), BF16),
        D((3,)),
        V((spots, blocks_dev), BF16), V((blocks_dev, spots), BF16),
        V((spots, 2 * pairs), BF16), V((pairs, spots), BF16),
        V((slabs, 2 * pairs), BF16), V((pairs, 2 * slabs), BF16),
        V((owners, cap, LANES), F32), V((owners, cap, LANES), F32),
        V((9 * blocks_dev // 2, LANES), F32),
        V((blocks_dev, COLS), F32), V((blocks_dev, COLS), F32), V((blocks_dev, COLS), F32),
        V((blocks_dev, COLS), F32),
        V((ITERS, owners, cap, COLS), F32), V((ITERS, owners, cap, COLS), F32),
        V((5, pairs, LANES), F32),
        V((2, pairs, points), F32),
        V((6, 2 * pairs, width), BF16),
        V((3, pairs, width), F32),
        V((2, 144, width), BF16),
        V((pairs // 8, 2, 144, 4 * BLOCK), F32),
        V((pairs, COLS), F32),
        V((CHUNKS, 2, nx, 6, slabs, part), F32), V((CHUNKS, nx, 6, slabs, part), F32),
        V((CHUNKS, nx, 6, slabs, part), F32), V((CHUNKS, far, 6, slabs, part), F32),
        V((CHUNKS, 6, slabs, part), F32),
        V((ITERS, CHUNKS, 2, nx, 3, slabs, part), F32), V((ITERS, CHUNKS, nx, 3, slabs, part), F32),
        V((ITERS, CHUNKS, nx, 3, slabs, part), F32), V((ITERS, CHUNKS, far, 3, slabs, part), F32),
        V((ITERS, CHUNKS, 2, nx, 3, slabs, part), F32),
        V((ITERS, owners, cap, COLS), F32), V((ITERS, owners, cap, COLS), F32),
        V((3, 2, 8, LANES), F32), V((3, owners - 1, 2, 8, LANES), F32),
        V((3, ncam, 2, 8, LANES), F32),
        D((owners - 1,)), D((owners - 1,)),
        D((ITERS, owners - 1)), D((ITERS, owners - 1)),
        D((ITERS, owners - 1)), D((ITERS, owners - 1)),
        D((2, CHUNKS)), D((2, CHUNKS, far)),
        D((ITERS, 2, CHUNKS)), D((ITERS, 2, CHUNKS, far)),
        D((ITERS, 2, CHUNKS, far)), D((ITERS, 2, CHUNKS)),
        D((2, 3, owners - 1)), D((2, 3, ncam - 1)),
    ]
    return pl.pallas_call(
        body,
        name="cg",
        out_shape=[jax.ShapeDtypeStruct((9, cam_dev), F32)] * 2,
        in_specs=[vmem] * 6 + [hbm] * 3,
        out_specs=[vmem] * 2,
        scratch_shapes=scratch,
        compiler_params=pltpu.CompilerParams(
            collective_id=0, has_side_effects=True, vmem_limit_bytes=VMEM_BYTES
        ),
    )(
        block_ids.reshape(1, pairs), slab_ids.reshape(1, pairs), pair_count.reshape(1, 1),
        right_side, cam_damping, point_damping.reshape(-1, LANES), idx, jc, jp,
    )


def solution(mesh):
    in_specs = (
        P(None, ("cam", "pt")),
        P(None, ("cam", "pt")),
        P("pt"),
        P("cam", "pt", None),
        P("cam", "pt", None),
        P("cam", "pt", None, None),
        P("cam", "pt", None, None, None),
        P("cam", "pt", None, None, None),
        P("cam", "pt"),
    )
    out_specs = (P(None, ("cam", "pt")), P(None, ("cam", "pt")))
    return jax.shard_map(
        per_device, mesh=mesh, in_specs=in_specs, out_specs=out_specs, check_vma=False
    )
```

time: 269 us -> 127 us (0.47)
  Pallas kernels: 243 us -> 122 us
  local copies, waits for them, and re-layouts: 12.1 us -> 3.14 us
  other arithmetic: 8.33 us -> 0 us
    pallas_call x17 -> x1, Pallas kernels: 243 us -> 122 us  [per_device(): pl.pallas_call(body, name='cg', out_shape=[jax.ShapeDtypeStruct((9, cam_d...]
    unnamed x26 -> x2, local copies, waits for them, and re-layouts: 9.89 us -> 3.14 us
    reduce_sum x9 -> x0, other arithmetic: 4.35 us -> none  [the longest x2 1.3 us: over_pt(): return jnp.sum(swap(tile_of([value]), 'pt', True, 5)[:, 0, 0, 0])]
    another operation x9 -> x0, other arithmetic: 3.01 us -> none  [the longest x3 2.76 us: tile_of(): jnp.stack(values)[:, None, None]]
where the time goes in v1:
time: 127 us
  Pallas kernels  122 us (96%)
  local copies, waits for them, and re-layouts  3.14 us (2%)
  between operations  1.29 us (1%)
    pallas_call x1, Pallas kernels, per_device(): pl.pallas_call(body, name='cg', out_shape=[jax.ShapeDtypeStruct((9, cam_d...  122 us
    unnamed x2, local copies, waits for them, and re-layouts  3.14 us

profile of v1, /device:TPU:0, one launch (start us, length us, event | category | flops | bytes accessed | tf_op | source)
XLA Modules:
  0.0 126.9 jit_solution(12939895207084903824)
XLA Ops:
  1.3 122.5 %cg.1 = (f32[9,2048]{1,0:T(8,128)}, f32[9,2048]{1,0:T(8,128)}) custom-call(s32[1,64]{1,0:T(1,128)} %bitcast.14, s32[1,64]{1,0:T(1,128)} %bitcast.15, s32[1,1]{1,0:T(1,128)S(6)} %copy.13.count_ref, f32[9,2048]{1,0:T(8,128)} %rs_ref.1, f32[9,2048]{1,0:T(8,128)} %damp_ref.1, f32[512,128]{1,0:T(8,128)} %bitcast.13, s32[64,4096]{1,0:T(8,128)} %bitcast.12, ...), custom_call_target="tpu_custom_call" | custom-call | tf_op jit(solution)/shard_map/cg/pallas_call | solution.py:631
  123.8 1.6 %copy.14 = f32[9,2048]{1,0:T(8,128)} copy(f32[9,2048]{1,0:T(8,128)} %get-tuple-element.4) | data formatting | bytes 147456
  125.3 1.6 %copy.15 = f32[9,2048]{1,0:T(8,128)} copy(f32[9,2048]{1,0:T(8,128)} %get-tuple-element.5) | data formatting | bytes 147456

commit v2 on v1

--- a/solution.py
+++ b/solution.py
@@ -12,6 +12,7 @@
 LANES = 128
 CHUNKS = 4
 COLS = 5 * LANES
+KCOLS = 4 * LANES
 F32 = jnp.float32
 BF16 = jnp.bfloat16
 VMEM_BYTES = 60 * 1024 * 1024
@@ -67,7 +68,7 @@
 def body(
     ids_ref, slab_ref, count_ref, rs_ref, damp_ref, pdamp_ref, idx_hbm, jc_hbm, jp_hbm,
     answer_ref, residual_ref,
-    idx, jc, jp, load_sem,
+    idx, jc, jp, hots, load_sem,
     place, place_t, pick, pick_t, sums_by_slab, slab_hot_t, asks_mine, asks,
     flat, v0, v1, v2, damp, packed, got, tables, proj, tbuf, zslot, pbuf, acc, slotsum,
     h_part, h_sib, h_red, h_far, inverse, y_part, y_sib, y_red, y_far, z_all,
@@ -176,15 +177,9 @@
         for i in range(5):
             even = value[0:half, i * LANES : (i + 1) * LANES]
             odd = value[half:, i * LANES : (i + 1) * LANES]
-            flat[pl.ds(2 * i * half, half), :] = jnp.where(low_lane, even, pltpu.roll(odd, BLOCK, 1))
+            target[2 * i] = jnp.where(low_lane, even, pltpu.roll(odd, BLOCK, 1))
             if i < 4:
-                flat[pl.ds((2 * i + 1) * half, half), :] = jnp.where(
-                    low_lane, pltpu.roll(even, BLOCK, 1), odd
-                )
-        for r in range(half):
-            cols = pl.ds(r * LANES, LANES)
-            target[0:8, cols] = flat[pl.ds(r, 8, stride=half), :]
-            target[8:9, cols] = flat[8 * half + r : 8 * half + r + 1, :]
+                target[2 * i + 1] = jnp.where(low_lane, pltpu.roll(even, BLOCK, 1), odd)
 
     to_rows(rs_ref, v0)
     to_rows(damp_ref, damp)
@@ -263,20 +258,63 @@
     place[...] = hot[:, : 2 * half].astype(BF16)
     place_t[...] = hot.T[: 2 * half, :].astype(BF16)
 
+    short_low = iota((cap // 2, LANES), 1) < BLOCK
+
+    def pack(value, buf):
+        for o in range(owners):
+            rows = value[o * cap : (o + 1) * cap]
+            for i in range(4):
+                buf[o, i * cap : (i + 1) * cap, :] = rows[:, i * LANES : (i + 1) * LANES]
+            last = rows[:, 4 * LANES :]
+            buf[o, 4 * cap :, :] = jnp.where(
+                short_low, last[: cap // 2], pltpu.roll(last[cap // 2 :], BLOCK, 1)
+            )
+
+    def unpack(buf):
+        tall = []
+        for o in range(owners):
+            cols = [buf[o, i * cap : (i + 1) * cap, :] for i in range(4)]
+            last = buf[o, 4 * cap :, :]
+            zero = jnp.zeros_like(last)
+            last = [
+                jnp.where(short_low, last, zero),
+                jnp.where(short_low, pltpu.roll(last, BLOCK, 1), zero),
+            ]
+            cols.append(jnp.concatenate(last, axis=0))
+            tall.append(jnp.concatenate(cols, axis=1))
+        return jnp.concatenate(tall, axis=0)
+
     def send_blocks(vec, it):
-        out = select_rows(place[...], vec[...])
-        packed[it] = out.reshape(owners, cap, COLS)
+        pack(select_rows(place[...], vec[...]), packed.at[it])
         got[it, me_pt] = packed[it, me_pt]
         return pt_exchange(
             lambda peer: packed.at[it, peer], got.at[it], a_send.at[it], a_recv.at[it]
         )
 
     def make_tables(it):
-        value = select_rows(pick_t[...], got[it].reshape(spots, COLS))
+        value = select_rows(pick_t[...], unpack(got.at[it]))
         for i in range(5):
-            tables[i] = value[:, i * LANES : (i + 1) * LANES]
+            here = value[:, i * LANES : (i + 1) * LANES]
+            tables[2 * i] = here
+            if i < 4:
+                tables[2 * i + 1] = pltpu.roll(here, BLOCK, 1)
 
     a_copies = send_blocks(v0, 0)
+
+    loads[1].wait()
+
+    def hot_tile(t, carry):
+        cols = pl.ds(pl.multiple_of(t * LANES, LANES), LANES)
+        cams = iota((BLOCK // 2, LANES), 0)
+        here = idx[:, cols] & (BLOCK // 2 - 1)
+        for j in range(pairs):
+            line = jnp.broadcast_to(here[j : j + 1, :], (BLOCK // 2, LANES))
+            hots[j * BLOCK // 2 : (j + 1) * BLOCK // 2, cols] = jnp.where(
+                cams == line, 1.0, 0.0
+            ).astype(BF16)
+        return carry
+
+    lax.fori_loop(0, points // LANES, hot_tile, 0)
 
     h_far_copies = []
     for c in range(CHUNKS):
@@ -308,12 +346,11 @@
             spot = pl.ds(pl.multiple_of(t * LANES, LANES), LANES)
             for g in range(pairs // 16):
                 rows = slice(g * 16, g * 16 + 16)
-                index = [idx[rows, cols]]
-                index.append(index[0] + BLOCK)
+                index = idx[rows, cols]
                 pr = [None, None]
                 for k in range(9):
                     at_camera = jnp.take_along_axis(
-                        tables[k // 2, rows, :], index[k % 2], axis=1, mode="promise_in_bounds"
+                        tables[k, rows, :], index, axis=1, mode="promise_in_bounds"
                     )
                     for i in range(2):
                         term = jc[9 * i + k, rows, cols].astype(F32) * at_camera
@@ -375,7 +412,7 @@
                     slab_hot_t[...], jnp.concatenate([high, low], axis=0)
                 )
 
-        def group(g, carry):
+        def build(g):
             base = pl.multiple_of(g * 16, 16)
             rows = pl.ds(base, 16)
             for t in range(width // LANES):
@@ -391,70 +428,80 @@
                     + jc[9 + k, rows, cols].astype(F32) * miss[1]
                     for k in range(9)
                 ]
+                upper = jnp.where(idx[rows, cols] >= BLOCK // 2, 1.0, 0.0)
                 for h in range(2):
                     mine = [value[h * 8 : h * 8 + 8] for value in push]
                     last_high = mine[8].astype(BF16).astype(F32)
+                    halves = upper[h * 8 : h * 8 + 8]
+                    halves = jnp.concatenate([halves, halves], axis=0).astype(BF16) > 0.5
+                    tiles = [None] * 9
                     for i in range(4):
                         pair = jnp.concatenate([mine[2 * i], mine[2 * i + 1]], axis=0)
-                        high, low = split2(pair)
-                        pbuf[h, 16 * i : 16 * i + 16, spot] = high
-                        pbuf[h, 80 + 16 * i : 96 + 16 * i, spot] = low
+                        tiles[i], tiles[5 + i] = split2(pair)
                     pair = jnp.concatenate([last_high, mine[8] - last_high], axis=0)
-                    pbuf[h, 64:80, spot] = pair.astype(BF16)
-            cams = iota((BLOCK, 2 * LANES), 0)
+                    tiles[4] = pair.astype(BF16)
+                    for i, value in enumerate(tiles):
+                        pbuf[h, 16 * i : 16 * i + 16, spot] = value
+                        above = jnp.where(halves, value, jnp.zeros_like(value))
+                        pbuf[h, 144 + 16 * i : 160 + 16 * i, spot] = above
+
+        def scatter(g):
+            base = g * 16
             for h in range(2):
-                for s in range(2):
-                    total = None
-                    for t in range(width // (2 * LANES)):
-                        cols = pl.ds(c * width + t * 2 * LANES, 2 * LANES)
-                        here = idx[pl.ds(pl.multiple_of(base + h * 8, 8), 8), cols]
-                        hots = []
-                        for j in range(4):
-                            line = here[s * 4 + j : s * 4 + j + 1, :]
-                            line = jnp.broadcast_to(line, (BLOCK, 2 * LANES))
-                            hots.append(jnp.where(cams == line, 1.0, 0.0).astype(BF16))
-                        piece = lax.dot_general(
-                            pbuf[h, :, t * 2 * LANES : (t + 1) * 2 * LANES],
-                            jnp.concatenate(hots, axis=0),
-                            (((1,), (1,)), ((), ())),
-                            preferred_element_type=F32,
-                        )
-                        total = piece if total is None else total + piece
-                    if c == 0:
-                        acc[2 * g + h, s] = total
-                    else:
-                        acc[2 * g + h, s] += total
+                total = None
+                for t in range(width // KCOLS):
+                    cols = pl.ds(c * width + t * KCOLS, KCOLS)
+                    hot_rows = pl.ds(pl.multiple_of((base + h * 8) * (BLOCK // 2), 256), 4 * BLOCK)
+                    piece = lax.dot_general(
+                        pbuf[h, :, t * KCOLS : (t + 1) * KCOLS],
+                        hots[hot_rows, cols],
+                        (((1,), (1,)), ((), ())),
+                        preferred_element_type=F32,
+                    )
+                    total = piece if total is None else total + piece
+                if c == 0:
+                    acc[2 * g + h] = total
+                else:
+                    acc[2 * g + h] += total
+
+        groups = pairs // 16
+
+        def group(g, carry):
+            build(g)
+            scatter(g)
             return carry
 
-        lax.fori_loop(0, pairs // 16, group, 0)
+        lax.fori_loop(0, groups, group, 0)
 
     def slot_sums():
         small = (8, LANES)
         row = iota(small, 0)
+        quarter = iota(small, 1) // (BLOCK // 2)
         first4 = row < 4
-        right = lax.rem(row, 4) >= 2
-        odd = lax.rem(row, 2) == 1
-        low8 = iota(small, 1) < BLOCK
+        turn = lax.rem(row, 4)
 
         def one(g, carry):
-            lows, highs = [], []
-            for f in range(9):
-                other = 72 if f == 8 else 80 + 8 * f
-                cut = []
-                for s in range(2):
-                    cut.append(acc[g, s, 8 * f : 8 * f + 8, :] + acc[g, s, other : other + 8, :])
-                here = jnp.where(
-                    right,
-                    jnp.where(first4, cut[0][:, LANES:], cut[1][:, LANES:]),
-                    jnp.where(first4, cut[0][:, :LANES], cut[1][:, :LANES]),
-                )
-                turned = pltpu.roll(here, BLOCK, 1)
-                lows.append(jnp.where(odd, turned, here))
-                highs.append(jnp.where(odd, here, turned))
             rows = pl.ds(pl.multiple_of(g * 8, 8), 8)
             for i in range(5):
-                high = highs[2 * i + 1] if i < 4 else jnp.zeros(small, F32)
-                slotsum[rows, i * LANES : (i + 1) * LANES] = jnp.where(low8, lows[2 * i], high)
+                line = jnp.zeros(small, F32)
+                for q in range(4 if i < 4 else 2):
+                    f = 2 * i + q // 2
+                    if q % 2 == 0:
+                        parts = []
+                        for top in (0, 144):
+                            low = top + (72 if f == 8 else 80 + 8 * f)
+                            parts.append(
+                                acc[g, top + 8 * f : top + 8 * f + 8, :] + acc[g, low : low + 8, :]
+                            )
+                    both = parts[0] - parts[1] if q % 2 == 0 else parts[1]
+                    here = jnp.where(first4, both[:, :LANES], both[:, LANES:])
+                    moved = None
+                    for k in range(4):
+                        shift = (32 * (q - k)) % LANES
+                        turned = pltpu.roll(here, shift, 1) if shift else here
+                        moved = turned if k == 0 else jnp.where(turn == k, turned, moved)
+                    line = jnp.where(quarter == q, moved, line)
+                slotsum[rows, i * LANES : (i + 1) * LANES] = line
             return carry
 
         lax.fori_loop(0, pairs // 8, one, 0)
@@ -464,10 +511,9 @@
         make_tables(it)
         next(beside, None)
         if it == 0:
-            loads[1].wait()
             loads[2].wait()
         first, second, third, fourth = {}, {}, {}, {}
-        for step in range(CHUNKS + 3):
+        for step in range(CHUNKS + 4):
             if step < CHUNKS:
                 first[step] = forward(step, it)
                 next(beside, None)
@@ -477,19 +523,18 @@
                 third[step - 2] = eliminate(step - 2, it, second[step - 2])
             if 0 <= step - 3 < CHUNKS:
                 fourth[step - 3] = share(step - 3, it, third[step - 3])
-            if step - 3 >= 0 and step >= CHUNKS - 1:
-                backward(step - 3, it, fourth[step - 3])
+            if step - 4 >= 0:
+                backward(step - 4, it, fourth[step - 4])
         slot_sums()
         next(beside, None)
         high, low = split2(slotsum[...])
-        out = dot(pick[...], jnp.concatenate([high, low], axis=0))
-        out_pack[it] = out.reshape(owners, cap, COLS)
+        pack(dot(pick[...], jnp.concatenate([high, low], axis=0)), out_pack.at[it])
         in_pack[it, me_pt] = out_pack[it, me_pt]
         copies = pt_exchange(
             lambda peer: out_pack.at[it, peer], in_pack.at[it], e_send.at[it], e_recv.at[it]
         )
         wait_all(copies)
-        high, low = split2(in_pack[it].reshape(spots, COLS))
+        high, low = split2(unpack(in_pack.at[it]))
         total = dot(place_t[...], high) + dot(place_t[...], low)
         return damp[...] * vec[...] + total
 
@@ -595,6 +640,7 @@
     far = max(nx - 1, 1)
     scratch = [
         V((pairs, points), jnp.int32), V((18, pairs, points), BF16), V((6, pairs, points), BF16),
+        V((pairs * BLOCK // 2, points), BF16),
         D((3,)),
         V((spots, blocks_dev), BF16), V((blocks_dev, spots), BF16),
         V((spots, 2 * pairs), BF16), V((pairs, spots), BF16),
@@ -603,13 +649,14 @@
         V((9 * blocks_dev // 2, LANES), F32),
         V((blocks_dev, COLS), F32), V((blocks_dev, COLS), F32), V((blocks_dev, COLS), F32),
         V((blocks_dev, COLS), F32),
-        V((ITERS, owners, cap, COLS), F32), V((ITERS, owners, cap, COLS), F32),
-        V((5, pairs, LANES), F32),
+        V((ITERS, owners, 4 * cap + cap // 2, LANES), F32),
+        V((ITERS, owners, 4 * cap + cap // 2, LANES), F32),
+        V((9, pairs, LANES), F32),
         V((2, pairs, points), F32),
         V((6, 2 * pairs, width), BF16),
         V((3, pairs, width), F32),
-        V((2, 144, width), BF16),
-        V((pairs // 8, 2, 144, 4 * BLOCK), F32),
+        V((2, 288, width), BF16),
+        V((pairs // 8, 288, 4 * BLOCK), F32),
         V((pairs, COLS), F32),
         V((CHUNKS, 2, nx, 6, slabs, part), F32), V((CHUNKS, nx, 6, slabs, part), F32),
         V((CHUNKS, nx, 6, slabs, part), F32), V((CHUNKS, far, 6, slabs, part), F32),
@@ -617,7 +664,8 @@
         V((ITERS, CHUNKS, 2, nx, 3, slabs, part), F32), V((ITERS, CHUNKS, nx, 3, slabs, part), F32),
         V((ITERS, CHUNKS, nx, 3, slabs, part), F32), V((ITERS, CHUNKS, far, 3, slabs, part), F32),
         V((ITERS, CHUNKS, 2, nx, 3, slabs, part), F32),
-        V((ITERS, owners, cap, COLS), F32), V((ITERS, owners, cap, COLS), F32),
+        V((ITERS, owners, 4 * cap + cap // 2, LANES), F32),
+        V((ITERS, owners, 4 * cap + cap // 2, LANES), F32),
         V((3, 2, 8, LANES), F32), V((3, owners - 1, 2, 8, LANES), F32),
         V((3, ncam, 2, 8, LANES), F32),
         D((owners - 1,)), D((owners - 1,)),
@@ -628,10 +676,10 @@
         D((ITERS, 2, CHUNKS, far)), D((ITERS, 2, CHUNKS)),
         D((2, 3, owners - 1)), D((2, 3, ncam - 1)),
     ]
-    return pl.pallas_call(
+    outs = pl.pallas_call(
         body,
         name="cg",
-        out_shape=[jax.ShapeDtypeStruct((9, cam_dev), F32)] * 2,
+        out_shape=[jax.ShapeDtypeStruct((9, blocks_dev // 2, LANES), F32)] * 2,
         in_specs=[vmem] * 6 + [hbm] * 3,
         out_specs=[vmem] * 2,
         scratch_shapes=scratch,
@@ -642,6 +690,7 @@
         block_ids.reshape(1, pairs), slab_ids.reshape(1, pairs), pair_count.reshape(1, 1),
         right_side, cam_damping, point_damping.reshape(-1, LANES), idx, jc, jp,
     )
+    return outs[0].reshape(9, cam_dev), outs[1].reshape(9, cam_dev)
 
 
 def solution(mesh):

time: 127 us -> 115 us (0.906)
  Pallas kernels: 122 us -> 111 us
    pallas_call x1, Pallas kernels: 122 us -> 111 us  [per_device(): pl.pallas_call(body, name='cg', out_shape=[jax.ShapeDtypeStruct((9, block...]
    unnamed x2 -> x4, local copies, waits for them, and re-layouts: 3.14 us -> 3.18 us
where the time goes in v2:
time: 115 us
  Pallas kernels  111 us (97%)
  local copies, waits for them, and re-layouts  3.18 us (3%)
  between operations  1.29 us (1%)
    pallas_call x1, Pallas kernels, per_device(): pl.pallas_call(body, name='cg', out_shape=[jax.ShapeDtypeStruct((9, block...  111 us
    unnamed x4, local copies, waits for them, and re-layouts  3.18 us

profile of v2, /device:TPU:0, one launch (start us, length us, event | category | flops | bytes accessed | tf_op | source)
XLA Modules:
  0.0 115.2 jit_solution(8986763742792340973)
XLA Ops:
  1.3 110.7 %cg.1 = (f32[9,16,128]{2,1,0:T(8,128)}, f32[9,16,128]{2,1,0:T(8,128)}) custom-call(s32[1,64]{1,0:T(1,128)} %bitcast.24, s32[1,64]{1,0:T(1,128)} %bitcast.25, s32[1,1]{1,0:T(1,128)S(6)} %copy.13.count_ref, f32[9,2048]{1,0:T(8,128)} %rs_ref.1, f32[9,2048]{1,0:T(8,128)} %damp_ref.1, f32[512,128]{1,0:T(8,128)} %bitcast.21, s32[64,4096]{1,0:T(8,128)} %bitcast.18, ...), custom_call_target="tpu_custom_call" | custom-call | tf_op jit(solution)/shard_map/cg/pallas_call | solution.py:679
  112.0 0.9 pad
  112.9 0.7 copy.11
  113.6 0.9 pad.1
  114.5 0.7 copy.12

commit v3 on v2

--- a/solution.py
+++ b/solution.py
@@ -102,13 +102,16 @@
     def at_pt(pt):
         return {"pt": pt}
 
-    loads = [
-        pltpu.make_async_copy(jp_hbm, jp, load_sem.at[0]),
-        pltpu.make_async_copy(idx_hbm, idx, load_sem.at[1]),
-        pltpu.make_async_copy(jc_hbm, jc, load_sem.at[2]),
-    ]
-    for copy in loads:
+    def load(source, target, sem, c):
+        cols = pl.ds(c * width, width)
+        copy = pltpu.make_async_copy(source.at[:, :, cols], target.at[:, :, cols], sem)
         copy.start()
+        return copy
+
+    jp_loads = [load(jp_hbm, jp, load_sem.at[c], c) for c in range(CHUNKS)]
+    idx_load = pltpu.make_async_copy(idx_hbm, idx, load_sem.at[2 * CHUNKS])
+    idx_load.start()
+    jc_loads = [load(jc_hbm, jc, load_sem.at[CHUNKS + c], c) for c in range(CHUNKS)]
 
     barrier = pltpu.get_barrier_semaphore()
     for hop in range(1, owners):
@@ -191,7 +194,7 @@
         for hop in range(1, owners):
             peer = lax.rem(me_pt + hop, owners)
             copy = pltpu.make_async_remote_copy(
-                src_ref=sources(peer), dst_ref=target.at[me_pt],
+                src_ref=sources(peer), dst_ref=target,
                 send_sem=send_sem.at[hop - 1], recv_sem=recv_sem.at[hop - 1],
                 device_id=at_pt(peer), device_id_type=MESH,
             )
@@ -203,7 +206,7 @@
         for copy in copies:
             copy.wait()
 
-    ask_copies = pt_exchange(lambda peer: asks_mine.at[peer], asks, ask_send, ask_recv)
+    ask_copies = pt_exchange(lambda peer: asks_mine.at[peer], asks.at[me_pt], ask_send, ask_recv)
     asks[me_pt] = asks_mine[me_pt]
 
     def to_sibling(source, target, sems, c):
@@ -231,44 +234,19 @@
         for q in range(ncam):
             buf[c, q % 2, q // 2, k] = value[:, q * part : (q + 1) * part]
 
-    loads[0].wait()
-    h_copies = []
-    for c in range(CHUNKS):
-
-        def hess_tile(t, carry, c=c):
-            col = pl.multiple_of(c * width + t * LANES, LANES)
-            spot = pl.ds(pl.multiple_of(t * LANES, LANES), LANES)
-            for g in range(pairs // 16):
-                rows = slice(g * 16, g * 16 + 16)
-                point = [jp[k, rows, pl.ds(col, LANES)].astype(F32) for k in range(6)]
-                for f, (a, b) in enumerate(HESS):
-                    high, low = split2(point[a] * point[b] + point[3 + a] * point[3 + b])
-                    tbuf[f, rows, spot] = high
-                    tbuf[f, pairs + g * 16 : pairs + g * 16 + 16, spot] = low
-            return carry
-
-        lax.fori_loop(0, width // LANES, hess_tile, 0)
-        for f in range(6):
-            put_parts(h_part, c, f, dot(sums_by_slab[...], tbuf[f]))
-        h_copies.append(to_sibling(h_part.at[c, 1 - me_core], h_sib.at[c], hs_sem, c))
-
-    wait_all(ask_copies)
-    wanted = asks[...].reshape(spots, LANES)
-    hot = jnp.where(wanted == lane.astype(F32), 1.0, 0.0)
-    place[...] = hot[:, : 2 * half].astype(BF16)
-    place_t[...] = hot.T[: 2 * half, :].astype(BF16)
-
     short_low = iota((cap // 2, LANES), 1) < BLOCK
 
-    def pack(value, buf):
+    def pack(value, buf, first, last):
         for o in range(owners):
             rows = value[o * cap : (o + 1) * cap]
-            for i in range(4):
-                buf[o, i * cap : (i + 1) * cap, :] = rows[:, i * LANES : (i + 1) * LANES]
-            last = rows[:, 4 * LANES :]
-            buf[o, 4 * cap :, :] = jnp.where(
-                short_low, last[: cap // 2], pltpu.roll(last[cap // 2 :], BLOCK, 1)
-            )
+            for i in range(first, last):
+                part_of = rows[:, (i - first) * LANES : (i - first + 1) * LANES]
+                if i < 4:
+                    buf[o, i * cap : (i + 1) * cap, :] = part_of
+                else:
+                    buf[o, 4 * cap :, :] = jnp.where(
+                        short_low, part_of[: cap // 2], pltpu.roll(part_of[cap // 2 :], BLOCK, 1)
+                    )
 
     def unpack(buf):
         tall = []
@@ -285,10 +263,10 @@
         return jnp.concatenate(tall, axis=0)
 
     def send_blocks(vec, it):
-        pack(select_rows(place[...], vec[...]), packed.at[it])
+        pack(select_rows(place[...], vec[...]), packed.at[it], 0, 5)
         got[it, me_pt] = packed[it, me_pt]
         return pt_exchange(
-            lambda peer: packed.at[it, peer], got.at[it], a_send.at[it], a_recv.at[it]
+            lambda peer: packed.at[it, peer], got.at[it, me_pt], a_send.at[it], a_recv.at[it]
         )
 
     def make_tables(it):
@@ -299,9 +277,43 @@
             if i < 4:
                 tables[2 * i + 1] = pltpu.roll(here, BLOCK, 1)
 
-    a_copies = send_blocks(v0, 0)
-
-    loads[1].wait()
+    h_copies = []
+    for c in range(CHUNKS):
+        jp_loads[c].wait()
+        if c == CHUNKS // 2:
+            wait_all(ask_copies)
+            wanted = asks[...].reshape(spots, LANES)
+            hot = jnp.where(wanted == lane.astype(F32), 1.0, 0.0)
+            place[...] = hot[:, : 2 * half].astype(BF16)
+            place_t[...] = hot.T[: 2 * half, :].astype(BF16)
+            a_copies = send_blocks(v0, 0)
+
+        def hess_tile(t, carry, c=c):
+            col = pl.multiple_of(c * width + t * LANES, LANES)
+            spot = pl.ds(pl.multiple_of(t * LANES, LANES), LANES)
+            for g in range(pairs // 16):
+                rows = slice(g * 16, g * 16 + 16)
+                point = [jp[k, rows, pl.ds(col, LANES)].astype(F32) for k in range(6)]
+                for f, (a, b) in enumerate(HESS):
+                    high, low = split2(point[a] * point[b] + point[3 + a] * point[3 + b])
+                    tbuf[f, rows, spot] = high
+                    tbuf[f, pairs + g * 16 : pairs + g * 16 + 16, spot] = low
+            return carry
+
+        lax.fori_loop(0, width // LANES, hess_tile, 0)
+        for f in range(6):
+            put_parts(h_part, c, f, dot(sums_by_slab[...], tbuf[f]))
+        h_copies.append(to_sibling(h_part.at[c, 1 - me_core], h_sib.at[c], hs_sem, c))
+
+    h_far_copies = []
+    for c in range(CHUNKS):
+        wait_all(h_copies[c])
+        h_red[c] = h_part[c, me_core] + h_sib[c]
+        h_far_copies.append(
+            to_far(lambda peer: h_red.at[c, peer], lambda hop: h_far.at[c, hop - 1], hx_sem, c)
+        )
+
+    idx_load.wait()
 
     def hot_tile(t, carry):
         cols = pl.ds(pl.multiple_of(t * LANES, LANES), LANES)
@@ -315,14 +327,6 @@
         return carry
 
     lax.fori_loop(0, points // LANES, hot_tile, 0)
-
-    h_far_copies = []
-    for c in range(CHUNKS):
-        wait_all(h_copies[c])
-        h_red[c] = h_part[c, me_core] + h_sib[c]
-        h_far_copies.append(
-            to_far(lambda peer: h_red.at[c, peer], lambda hop: h_far.at[c, hop - 1], hx_sem, c)
-        )
 
     def finish_hessian(c):
         wait_all(h_far_copies[c])
@@ -340,6 +344,9 @@
                 inverse[c, f, :, cols] = value
 
     def forward(c, it):
+        if it == 0:
+            jc_loads[c].wait()
+
         def tile(t, carry):
             col = pl.multiple_of(c * width + t * LANES, LANES)
             cols = pl.ds(col, LANES)
@@ -473,7 +480,7 @@
 
         lax.fori_loop(0, groups, group, 0)
 
-    def slot_sums():
+    def slot_sums(first, last):
         small = (8, LANES)
         row = iota(small, 0)
         quarter = iota(small, 1) // (BLOCK // 2)
@@ -482,7 +489,7 @@
 
         def one(g, carry):
             rows = pl.ds(pl.multiple_of(g * 8, 8), 8)
-            for i in range(5):
+            for i in range(first, last):
                 line = jnp.zeros(small, F32)
                 for q in range(4 if i < 4 else 2):
                     f = 2 * i + q // 2
@@ -510,8 +517,6 @@
         wait_all(a_copies)
         make_tables(it)
         next(beside, None)
-        if it == 0:
-            loads[2].wait()
         first, second, third, fourth = {}, {}, {}, {}
         for step in range(CHUNKS + 4):
             if step < CHUNKS:
@@ -525,14 +530,20 @@
                 fourth[step - 3] = share(step - 3, it, third[step - 3])
             if step - 4 >= 0:
                 backward(step - 4, it, fourth[step - 4])
-        slot_sums()
+        copies = []
+        for n, (first, last) in enumerate(((0, 2), (2, 5))):
+            slot_sums(first, last)
+            high, low = split2(slotsum[:, first * LANES : last * LANES])
+            rows = slice(first * cap, last * cap if n == 0 else 4 * cap + cap // 2)
+            pack(
+                dot(pick[...], jnp.concatenate([high, low], axis=0)), out_pack.at[it], first, last
+            )
+            copies += pt_exchange(
+                lambda peer: out_pack.at[it, peer, rows], in_pack.at[it, me_pt, rows],
+                e_send.at[it, n], e_recv.at[it, n],
+            )
+        in_pack[it, me_pt] = out_pack[it, me_pt]
         next(beside, None)
-        high, low = split2(slotsum[...])
-        pack(dot(pick[...], jnp.concatenate([high, low], axis=0)), out_pack.at[it])
-        in_pack[it, me_pt] = out_pack[it, me_pt]
-        copies = pt_exchange(
-            lambda peer: out_pack.at[it, peer], in_pack.at[it], e_send.at[it], e_recv.at[it]
-        )
         wait_all(copies)
         high, low = split2(unpack(in_pack.at[it]))
         total = dot(place_t[...], high) + dot(place_t[...], low)
@@ -641,7 +652,7 @@
     scratch = [
         V((pairs, points), jnp.int32), V((18, pairs, points), BF16), V((6, pairs, points), BF16),
         V((pairs * BLOCK // 2, points), BF16),
-        D((3,)),
+        D((2 * CHUNKS + 1,)),
         V((spots, blocks_dev), BF16), V((blocks_dev, spots), BF16),
         V((spots, 2 * pairs), BF16), V((pairs, spots), BF16),
         V((slabs, 2 * pairs), BF16), V((pairs, 2 * slabs), BF16),
@@ -670,7 +681,7 @@
         V((3, ncam, 2, 8, LANES), F32),
         D((owners - 1,)), D((owners - 1,)),
         D((ITERS, owners - 1)), D((ITERS, owners - 1)),
-        D((ITERS, owners - 1)), D((ITERS, owners - 1)),
+        D((ITERS, 2, owners - 1)), D((ITERS, 2, owners - 1)),
         D((2, CHUNKS)), D((2, CHUNKS, far)),
         D((ITERS, 2, CHUNKS)), D((ITERS, 2, CHUNKS, far)),
         D((ITERS, 2, CHUNKS, far)), D((ITERS, 2, CHUNKS)),

time: 115 us -> 114 us (level)
    pallas_call x1, Pallas kernels: 111 us -> 110 us  [per_device(): pl.pallas_call(body, name='cg', out_shape=[jax.ShapeDtypeStruct((9, block...]
where the time goes in v3:
time: 114 us
  Pallas kernels  110 us (96%)
  local copies, waits for them, and re-layouts  3.18 us (3%)
  between operations  1.29 us (1%)
    pallas_call x1, Pallas kernels, per_device(): pl.pallas_call(body, name='cg', out_shape=[jax.ShapeDtypeStruct((9, block...  110 us
    unnamed x4, local copies, waits for them, and re-layouts  3.18 us

profile of v3, /device:TPU:0, one launch (start us, length us, event | category | flops | bytes accessed | tf_op | source)
XLA Modules:
  0.0 114.0 jit_solution(4250051022256259768)
XLA Ops:
  1.3 109.5 %cg.1 = (f32[9,16,128]{2,1,0:T(8,128)}, f32[9,16,128]{2,1,0:T(8,128)}) custom-call(s32[1,64]{1,0:T(1,128)} %bitcast.24, s32[1,64]{1,0:T(1,128)} %bitcast.25, s32[1,1]{1,0:T(1,128)S(6)} %copy.13.count_ref, f32[9,2048]{1,0:T(8,128)} %rs_ref.1, f32[9,2048]{1,0:T(8,128)} %damp_ref.1, f32[512,128]{1,0:T(8,128)} %bitcast.21, s32[64,4096]{1,0:T(8,128)} %bitcast.18, ...), custom_call_target="tpu_custom_call" | custom-call | tf_op jit(solution)/shard_map/cg/pallas_call | solution.py:690
  110.8 0.9 pad
  111.7 0.7 copy.11
  112.4 0.9 pad.1
  113.3 0.7 copy.12

commit v4 on v3

--- a/solution.py
+++ b/solution.py
@@ -300,7 +300,7 @@
                     tbuf[f, pairs + g * 16 : pairs + g * 16 + 16, spot] = low
             return carry
 
-        lax.fori_loop(0, width // LANES, hess_tile, 0)
+        lax.fori_loop(0, width // LANES, hess_tile, 0, unroll=2)
         for f in range(6):
             put_parts(h_part, c, f, dot(sums_by_slab[...], tbuf[f]))
         h_copies.append(to_sibling(h_part.at[c, 1 - me_core], h_sib.at[c], hs_sem, c))
@@ -374,7 +374,7 @@
                     tbuf[f, pairs + g * 16 : pairs + g * 16 + 16, spot] = low
             return carry
 
-        lax.fori_loop(0, width // LANES, tile, 0)
+        lax.fori_loop(0, width // LANES, tile, 0, unroll=2)
         for f in range(3):
             put_parts(y_part.at[it], c, f, dot(sums_by_slab[...], tbuf[f]))
         return to_sibling(

time: 114 us -> 112 us (0.982)
  Pallas kernels: 110 us -> 108 us
    pallas_call x1, Pallas kernels: 110 us -> 108 us  [per_device(): pl.pallas_call(body, name='cg', out_shape=[jax.ShapeDtypeStruct((9, block...]
where the time goes in v4:
time: 112 us
  Pallas kernels  108 us (96%)
  local copies, waits for them, and re-layouts  3.18 us (3%)
  between operations  1.29 us (1%)
    pallas_call x1, Pallas kernels, per_device(): pl.pallas_call(body, name='cg', out_shape=[jax.ShapeDtypeStruct((9, block...  108 us
    unnamed x4, local copies, waits for them, and re-layouts  3.18 us

profile of v4, /device:TPU:0, one launch (start us, length us, event | category | flops | bytes accessed | tf_op | source)
XLA Modules:
  0.0 112.2 jit_solution(7913627090206467966)
XLA Ops:
  1.3 107.8 %cg.1 = (f32[9,16,128]{2,1,0:T(8,128)}, f32[9,16,128]{2,1,0:T(8,128)}) custom-call(s32[1,64]{1,0:T(1,128)} %bitcast.24, s32[1,64]{1,0:T(1,128)} %bitcast.25, s32[1,1]{1,0:T(1,128)S(6)} %copy.13.count_ref, f32[9,2048]{1,0:T(8,128)} %rs_ref.1, f32[9,2048]{1,0:T(8,128)} %damp_ref.1, f32[512,128]{1,0:T(8,128)} %bitcast.21, s32[64,4096]{1,0:T(8,128)} %bitcast.18, ...), custom_call_target="tpu_custom_call" | custom-call | tf_op jit(solution)/shard_map/cg/pallas_call | solution.py:690
  109.0 0.9 pad
  109.9 0.7 copy.11
  110.6 0.9 pad.1
  111.5 0.7 copy.12
